TPU v7x, 32 devices: a whole 2x2x4 slice. The times are simulated.
32 devices in a mesh: dp: 8 (over y, x, core), tensor: 4 (over z).
Axes of the slice: x: 2, y: 2, z: 4, core: 2. Of those that a mesh axis runs over, the one named last changes fastest.
Arguments:
- picture_encoder_result: bfloat16 [2816, 1024], P('dp'), may hold values from -0.59765625 to 0.59765625
- sentence_encoder_result: bfloat16 [11264, 1024], P(('dp', 'tensor')), may hold values from -0.59765625 to 0.59765625
- picture_projector_matrix: bfloat16 [1024, 1024], P(None, 'tensor'), may hold values from -0.1875 to 0.1875
- sentence_projector_matrix: bfloat16 [1024, 1024], P(None, 'tensor'), may hold values from -0.1875 to 0.1875
- sentences_for_picture: int32 [2816], replicated, may hold values from 1 to 8, 11264 in all
- sharpness_factor: float32 [1], replicated, may hold values from 30 to 60
- score_offset_term: float32 [1], replicated, may hold values from -8 to -4
Outputs:
- grad_img: bfloat16 [2816, 1024], P('dp', 'tensor')
- grad_cap: bfloat16 [11264, 1024], P(('dp', 'tensor'))
Inputs may be any that keep to these rules, and one draw needn't show every extreme that they name: The counts sum to 11264; the captions of image m are the consecutive rows start[m] to start[m] + sentences_for_picture[m] - 1 of sentence_encoder_result, where start[m] is the sum of the counts of images before m; some image has 8.
All inputs are finite; a program needn't handle non-finite values.
Results may differ from a plain program's by a relative error of at most 0.014.
Values may be sent and summed in bfloat16 or wider, within the bound.
No kernel may reach another device: no remote copies, remote signals or barrier semaphores. Data moves between devices by JAX's collectives and lax.ppermute only.
A program may use at most 64 MiB of HBM per device.

v0:
```python
import jax
import jax.numpy as jnp
from jax import lax
from jax.sharding import PartitionSpec as P

epsilon = 1e-06


def passed_along(value, axis, steps):
    count = lax.axis_size(axis)
    pairs = [(source, (source + steps) % count) for source in range(count)]
    return lax.ppermute(value, axis, pairs)


def embed(features, loss_multiplier):
    raw = jnp.dot(features, loss_multiplier, preferred_element_type=jnp.float32)
    scale = lax.rsqrt(jnp.sum(raw * raw, axis=1, keepdims=True) + epsilon)
    return (raw * scale, scale)


def scaling_factor(
    similarity_matrix,
    other_begin_list,
    sentence_tally_later,
    other_position,
    scaled_sharpness,
    displacement,
):
    raw_similarity = scaled_sharpness * similarity_matrix + displacement
    inside = (other_position >= other_begin_list) & (
        other_position < other_begin_list + sentence_tally_later
    )
    match_polarity = jnp.where(inside, 1.0, -1.0)
    loss_multiplier = jnp.where(inside, 1.0 / sentence_tally_later.astype(jnp.float32), 1.0)
    return (
        scaled_sharpness
        * (-match_polarity * loss_multiplier * jax.nn.sigmoid(-match_polarity * raw_similarity))
    ).astype(jnp.bfloat16)


def unit_back(grad, unit, scale):
    return scale * (grad - unit * jnp.sum(unit * grad, axis=1, keepdims=True))


def divided_product(values, loss_multiplier):
    upper = lax.optimization_barrier(values.astype(jnp.bfloat16))
    lower = (values - upper.astype(jnp.float32)).astype(jnp.bfloat16)
    first = jnp.einsum("me,de->md", upper, loss_multiplier, preferred_element_type=jnp.float32)
    return first + jnp.einsum(
        "me,de->md", lower, loss_multiplier, preferred_element_type=jnp.float32
    )


def body(
    picture_encoder_result,
    sentence_encoder_result,
    picture_projector_matrix,
    sentence_projector_matrix,
    sentences_for_picture,
    sharpness_factor,
    score_offset_term,
):
    full_img, full_cap = (
        lax.all_gather(picture_projector_matrix, "tensor", axis=1, tiled=True),
        lax.all_gather(sentence_projector_matrix, "tensor", axis=1, tiled=True),
    )
    img_unit, img_scale = embed(picture_encoder_result, full_img)
    cap_unit, cap_scale = embed(sentence_encoder_result, full_cap)
    img_z = img_unit.astype(jnp.bfloat16)
    cap_z = cap_unit.astype(jnp.bfloat16)
    scaled_sharpness = sharpness_factor[0]
    displacement = score_offset_term[0]
    ends = jnp.cumsum(sentences_for_picture)
    starts = ends - sentences_for_picture
    cycle_count = lax.axis_size("dp")
    tensor_count = lax.axis_size("tensor")
    cycle_pos = lax.axis_index("dp")
    tensor_pos = lax.axis_index("tensor")
    img_rows = picture_encoder_result.shape[0]
    cap_rows = sentence_encoder_result.shape[0]
    width = img_z.shape[1]
    row_iota = jnp.arange(cap_rows, dtype=jnp.int32)
    sentence_number = (cycle_pos * tensor_count + tensor_pos) * cap_rows + row_iota

    def block_of(anchor):
        first = anchor * img_rows
        group_begin_list = lax.dynamic_slice_in_dim(starts, first, img_rows)
        group_sizes_list = lax.dynamic_slice_in_dim(sentences_for_picture, first, img_rows)
        return (group_begin_list, group_sizes_list)

    def image_tile(block_z, anchor):
        group_begin_list, group_sizes_list = block_of(anchor)
        similarity_matrix = jnp.einsum(
            "me,ce->mc", block_z, cap_z, preferred_element_type=jnp.float32
        )
        return scaling_factor(
            similarity_matrix,
            group_begin_list[:, None],
            group_sizes_list[:, None],
            sentence_number[None, :],
            scaled_sharpness,
            displacement,
        )

    own_starts, own_counts = block_of(cycle_pos)

    def caption_tile(cap_block, anchor):
        block_index = (anchor * tensor_count + tensor_pos) * cap_rows + row_iota
        scores_b = jnp.einsum("me,ce->mc", img_z, cap_block, preferred_element_type=jnp.float32)
        return scaling_factor(
            scores_b,
            own_starts[:, None],
            own_counts[:, None],
            block_index[None, :],
            scaled_sharpness,
            displacement,
        )

    def pair_work(turn, img_block, cap_block, img_grad, cap_grad):
        anchor = (cycle_pos - turn) % cycle_count
        coef_a = image_tile(img_block, anchor)
        cap_grad = cap_grad + jnp.einsum(
            "mc,me->ce", coef_a, img_block, preferred_element_type=jnp.float32
        )
        coef_b = caption_tile(cap_block, anchor)
        img_grad = img_grad + jnp.dot(coef_b, cap_block, preferred_element_type=jnp.float32)
        return (img_grad, cap_grad)

    def step(turn, state):
        img_block, cap_block, img_grad, cap_grad = state
        img_grad, cap_grad = pair_work(turn, img_block, cap_block, img_grad, cap_grad)
        img_block, cap_block = passed_along((img_block, cap_block), "dp", 1)
        return (img_block, cap_block, img_grad, cap_grad)

    start_state = (
        img_z,
        cap_z,
        jnp.zeros((img_rows, width), jnp.float32),
        jnp.zeros((cap_rows, width), jnp.float32),
    )
    img_block, cap_block, img_grad, cap_grad = lax.fori_loop(0, cycle_count - 1, step, start_state)
    img_grad, cap_grad = pair_work(cycle_count - 1, img_block, cap_block, img_grad, cap_grad)
    img_back = unit_back(img_grad, img_unit, img_scale)
    img_part = divided_product(img_back, full_img)
    grad_img = lax.psum_scatter(
        img_part.astype(jnp.bfloat16), "tensor", scatter_dimension=1, tiled=True
    )
    cap_back = unit_back(cap_grad, cap_unit, cap_scale)
    grad_cap = divided_product(cap_back, full_cap)
    return (grad_img, grad_cap.astype(jnp.bfloat16))


def solution(mesh):
    in_specs = (
        P("dp", None),
        P(("dp", "tensor"), None),
        P(None, "tensor"),
        P(None, "tensor"),
        P(),
        P(),
        P(),
    )
    out_specs = (P("dp", "tensor"), P(("dp", "tensor"), None))
    return jax.shard_map(body, mesh=mesh, in_specs=in_specs, out_specs=out_specs, check_vma=False)
```

profile of v0, /device:TPU:0, one launch (start us, length us, event | category | flops | bytes accessed | tf_op | source)
XLA Modules:
  0.0 283.5 jit_solution(3586098311252179926)
XLA Ops:
  8.0 0.7 all-gather.3.cloned.1.call-update
  8.8 1.0 reduce-window.9
  10.0 0.8 bitcast_subtract_fusion
  10.8 0.9 dynamic-slice_add_fusion.1
  11.6 0.8 broadcast_divide_fusion
  13.8 44.7 %all-gather.5.cloned.1.call-done = bf16[1024,1024]{1,0:T(8,128)(2,1)} async-done(((bf16[1024,256]{1,0:T(8,128)(2,1)}), bf16[1024,1024]{1,0:T(8,128)(2,1)}) %all-gather.5.cloned.1.call-update) | async-done | bytes 2097168 | tf_op jit(solution)/shard_map/all_gather | solution.py:65
  58.6 2.6 multiply_reduce_fusion.2
  61.2 43.4 %all-gather.3.cloned.1.call-done = bf16[1024,1024]{1,0:T(8,128)(2,1)} async-done(((bf16[1024,256]{1,0:T(8,128)(2,1)}), bf16[1024,1024]{1,0:T(8,128)(2,1)}) %all-gather.3.cloned.1.call-update) | async-done | bytes 2097168 | tf_op jit(solution)/shard_map/all_gather | solution.py:64
  104.6 2.6 multiply_reduce_fusion.3
  107.5 0.8 copy-done.3
  108.4 0.7 copy-done.7
  109.4 136.1 %while.22 = (s32[]{:T(128)}, bf16[352,1024]{1,0:T(8,128)(2,1)S(1)}, bf16[352,1024]{1,0:T(8,128)(2,1)S(1)}, f32[352,1024]{1,0:T(8,128)}, f32[352,1024]{1,0:T(8,12...) while((s32[]{:T(128)}, bf16[352,1024]{1,0:T(8,128)(2,1)S(1)}, ...), condition=%wide.region_5.6_spmd.clone, body=%wide.region_4.5_spmd.clone.sunk | while | flops 1020430464 | bytes 17330208 | solution.py:141
  109.5 0.9 copy.16
  110.4 1.6 collective-permute-start.1
  112.0 0.8 convert_divide_fusion.3
  112.8 0.8 dynamic-slice_add_fusion.4
  113.6 5.1 %convolution_add_fusion.8 = f32[352,1024]{1,0:T(8,128)} fusion(bf16[352,1024]{1,0:T(8,128)(2,1)} %copy.16, f32[352,1024]{1,0:T(8,128)} %get-tuple-element.665, bf16[352,1024]{1,0:T(8,128)(2,1)} %get-tuple-element.697, pred[]{:T(512)S(6)} %compare.5, f32[]{:T(128)} %get-tuple-element.698, f32[352]{0:T(512)S(1)} %divide_reduce_fusion.2, ...), kind=kOutput, calls=%fused_computation.3.clone.1 | convolution fusion | flops 510214144 | bytes 4331017 | tf_op jit(solution)/shard_map/while/body/eval_jaxpr/dot_general | solution.py:126
  118.7 4.8 %convolution_add_fusion.9 = f32[352,1024]{1,0:T(8,128)} fusion(bf16[352,1024]{1,0:T(8,128)(2,1)S(1)} %copy.15, f32[352,1024]{1,0:T(8,128)} %get-tuple-element.666, bf16[352,1024]{1,0:T(8,128)(2,1)} %get-tuple-element.701, pred[]{:T(512)S(6)} %compare.5, f32[352]{0:T(512)S(1)} %convert_divide_fusion.3, s32[352]{0:T(512)S(1)} %get-tuple-element.635, ...), kind=kOutput, calls=%fused_computation.2.clone.1 | convolution fusion | flops 510214144 | bytes 4331017 | tf_op jit(solution)/shard_map/while/body/eval_jaxpr/mc,me->ce/dot_general | solution.py:122
  123.5 5.4 %collective-permute-done.1 = bf16[352,1024]{1,0:T(8,128)(2,1)S(1)} collective-permute-done((bf16[352,1024]{1,0:T(8,128)(2,1)}, bf16[352,1024]{1,0:T(8,128)(2,1)S(1)}, u32[]{:S(2)}, u32[]{:S(2)}) %collective-permute-start.1) | collective-permute-done | bytes 720928 | tf_op jit(solution)/shard_map/while/body/eval_jaxpr/ppermute | solution.py:12
  129.0 0.9 copy.16
  130.5 0.8 convert_divide_fusion.3
  131.3 0.8 dynamic-slice_add_fusion.4
  132.1 5.6 %convolution_add_fusion.8 = f32[352,1024]{1,0:T(8,128)} fusion(bf16[352,1024]{1,0:T(8,128)(2,1)} %copy.16, f32[352,1024]{1,0:T(8,128)} %get-tuple-element.665, bf16[352,1024]{1,0:T(8,128)(2,1)} %get-tuple-element.697, pred[]{:T(512)S(6)} %compare.5, f32[]{:T(128)} %get-tuple-element.698, f32[352]{0:T(512)S(1)} %divide_reduce_fusion.2, ...), kind=kOutput, calls=%fused_computation.3.clone.1 | convolution fusion | flops 510214144 | bytes 4331017 | tf_op jit(solution)/shard_map/while/body/eval_jaxpr/dot_general | solution.py:126
  137.7 5.3 %convolution_add_fusion.9 = f32[352,1024]{1,0:T(8,128)} fusion(bf16[352,1024]{1,0:T(8,128)(2,1)S(1)} %copy.15, f32[352,1024]{1,0:T(8,128)} %get-tuple-element.666, bf16[352,1024]{1,0:T(8,128)(2,1)} %get-tuple-element.701, pred[]{:T(512)S(6)} %compare.5, f32[352]{0:T(512)S(1)} %convert_divide_fusion.3, s32[352]{0:T(512)S(1)} %get-tuple-element.635, ...), kind=kOutput, calls=%fused_computation.2.clone.1 | convolution fusion | flops 510214144 | bytes 4331017 | tf_op jit(solution)/shard_map/while/body/eval_jaxpr/mc,me->ce/dot_general | solution.py:122
  142.9 5.4 %collective-permute-done.1 = bf16[352,1024]{1,0:T(8,128)(2,1)S(1)} collective-permute-done((bf16[352,1024]{1,0:T(8,128)(2,1)}, bf16[352,1024]{1,0:T(8,128)(2,1)S(1)}, u32[]{:S(2)}, u32[]{:S(2)}) %collective-permute-start.1) | collective-permute-done | bytes 720928 | tf_op jit(solution)/shard_map/while/body/eval_jaxpr/ppermute | solution.py:12
  148.4 0.9 copy.16
  149.3 0.8 convert_divide_fusion.3
  150.1 0.8 dynamic-slice_add_fusion.4
  150.9 5.6 %convolution_add_fusion.8 = f32[352,1024]{1,0:T(8,128)} fusion(bf16[352,1024]{1,0:T(8,128)(2,1)} %copy.16, f32[352,1024]{1,0:T(8,128)} %get-tuple-element.665, bf16[352,1024]{1,0:T(8,128)(2,1)} %get-tuple-element.697, pred[]{:T(512)S(6)} %compare.5, f32[]{:T(128)} %get-tuple-element.698, f32[352]{0:T(512)S(1)} %divide_reduce_fusion.2, ...), kind=kOutput, calls=%fused_computation.3.clone.1 | convolution fusion | flops 510214144 | bytes 4331017 | tf_op jit(solution)/shard_map/while/body/eval_jaxpr/dot_general | solution.py:126
  156.4 5.3 %convolution_add_fusion.9 = f32[352,1024]{1,0:T(8,128)} fusion(bf16[352,1024]{1,0:T(8,128)(2,1)S(1)} %copy.15, f32[352,1024]{1,0:T(8,128)} %get-tuple-element.666, bf16[352,1024]{1,0:T(8,128)(2,1)} %get-tuple-element.701, pred[]{:T(512)S(6)} %compare.5, f32[352]{0:T(512)S(1)} %convert_divide_fusion.3, s32[352]{0:T(512)S(1)} %get-tuple-element.635, ...), kind=kOutput, calls=%fused_computation.2.clone.1 | convolution fusion | flops 510214144 | bytes 4331017 | tf_op jit(solution)/shard_map/while/body/eval_jaxpr/mc,me->ce/dot_general | solution.py:122
  161.7 6.0 %collective-permute-done.1 = bf16[352,1024]{1,0:T(8,128)(2,1)S(1)} collective-permute-done((bf16[352,1024]{1,0:T(8,128)(2,1)}, bf16[352,1024]{1,0:T(8,128)(2,1)S(1)}, u32[]{:S(2)}, u32[]{:S(2)}) %collective-permute-start.1) | collective-permute-done | bytes 720928 | tf_op jit(solution)/shard_map/while/body/eval_jaxpr/ppermute | solution.py:12
  167.8 0.9 copy.16
  168.8 0.8 convert_divide_fusion.3
  169.5 0.8 dynamic-slice_add_fusion.4
  170.3 5.6 %convolution_add_fusion.8 = f32[352,1024]{1,0:T(8,128)} fusion(bf16[352,1024]{1,0:T(8,128)(2,1)} %copy.16, f32[352,1024]{1,0:T(8,128)} %get-tuple-element.665, bf16[352,1024]{1,0:T(8,128)(2,1)} %get-tuple-element.697, pred[]{:T(512)S(6)} %compare.5, f32[]{:T(128)} %get-tuple-element.698, f32[352]{0:T(512)S(1)} %divide_reduce_fusion.2, ...), kind=kOutput, calls=%fused_computation.3.clone.1 | convolution fusion | flops 510214144 | bytes 4331017 | tf_op jit(solution)/shard_map/while/body/eval_jaxpr/dot_general | solution.py:126
  175.9 5.3 %convolution_add_fusion.9 = f32[352,1024]{1,0:T(8,128)} fusion(bf16[352,1024]{1,0:T(8,128)(2,1)S(1)} %copy.15, f32[352,1024]{1,0:T(8,128)} %get-tuple-element.666, bf16[352,1024]{1,0:T(8,128)(2,1)} %get-tuple-element.701, pred[]{:T(512)S(6)} %compare.5, f32[352]{0:T(512)S(1)} %convert_divide_fusion.3, s32[352]{0:T(512)S(1)} %get-tuple-element.635, ...), kind=kOutput, calls=%fused_computation.2.clone.1 | convolution fusion | flops 510214144 | bytes 4331017 | tf_op jit(solution)/shard_map/while/body/eval_jaxpr/mc,me->ce/dot_general | solution.py:122
  181.2 6.0 %collective-permute-done.1 = bf16[352,1024]{1,0:T(8,128)(2,1)S(1)} collective-permute-done((bf16[352,1024]{1,0:T(8,128)(2,1)}, bf16[352,1024]{1,0:T(8,128)(2,1)S(1)}, u32[]{:S(2)}, u32[]{:S(2)}) %collective-permute-start.1) | collective-permute-done | bytes 720928 | tf_op jit(solution)/shard_map/while/body/eval_jaxpr/ppermute | solution.py:12
  187.3 0.9 copy.16
  188.2 0.8 convert_divide_fusion.3
  189.0 0.8 dynamic-slice_add_fusion.4
  189.8 5.6 %convolution_add_fusion.8 = f32[352,1024]{1,0:T(8,128)} fusion(bf16[352,1024]{1,0:T(8,128)(2,1)} %copy.16, f32[352,1024]{1,0:T(8,128)} %get-tuple-element.665, bf16[352,1024]{1,0:T(8,128)(2,1)} %get-tuple-element.697, pred[]{:T(512)S(6)} %compare.5, f32[]{:T(128)} %get-tuple-element.698, f32[352]{0:T(512)S(1)} %divide_reduce_fusion.2, ...), kind=kOutput, calls=%fused_computation.3.clone.1 | convolution fusion | flops 510214144 | bytes 4331017 | tf_op jit(solution)/shard_map/while/body/eval_jaxpr/dot_general | solution.py:126
  195.3 5.3 %convolution_add_fusion.9 = f32[352,1024]{1,0:T(8,128)} fusion(bf16[352,1024]{1,0:T(8,128)(2,1)S(1)} %copy.15, f32[352,1024]{1,0:T(8,128)} %get-tuple-element.666, bf16[352,1024]{1,0:T(8,128)(2,1)} %get-tuple-element.701, pred[]{:T(512)S(6)} %compare.5, f32[352]{0:T(512)S(1)} %convert_divide_fusion.3, s32[352]{0:T(512)S(1)} %get-tuple-element.635, ...), kind=kOutput, calls=%fused_computation.2.clone.1 | convolution fusion | flops 510214144 | bytes 4331017 | tf_op jit(solution)/shard_map/while/body/eval_jaxpr/mc,me->ce/dot_general | solution.py:122
  200.6 6.0 %collective-permute-done.1 = bf16[352,1024]{1,0:T(8,128)(2,1)S(1)} collective-permute-done((bf16[352,1024]{1,0:T(8,128)(2,1)}, bf16[352,1024]{1,0:T(8,128)(2,1)S(1)}, u32[]{:S(2)}, u32[]{:S(2)}) %collective-permute-start.1) | collective-permute-done | bytes 720928 | tf_op jit(solution)/shard_map/while/body/eval_jaxpr/ppermute | solution.py:12
  206.7 0.9 copy.16
  207.6 0.8 convert_divide_fusion.3
  208.4 0.8 dynamic-slice_add_fusion.4
  209.2 5.6 %convolution_add_fusion.8 = f32[352,1024]{1,0:T(8,128)} fusion(bf16[352,1024]{1,0:T(8,128)(2,1)} %copy.16, f32[352,1024]{1,0:T(8,128)} %get-tuple-element.665, bf16[352,1024]{1,0:T(8,128)(2,1)} %get-tuple-element.697, pred[]{:T(512)S(6)} %compare.5, f32[]{:T(128)} %get-tuple-element.698, f32[352]{0:T(512)S(1)} %divide_reduce_fusion.2, ...), kind=kOutput, calls=%fused_computation.3.clone.1 | convolution fusion | flops 510214144 | bytes 4331017 | tf_op jit(solution)/shard_map/while/body/eval_jaxpr/dot_general | solution.py:126
  214.8 5.3 %convolution_add_fusion.9 = f32[352,1024]{1,0:T(8,128)} fusion(bf16[352,1024]{1,0:T(8,128)(2,1)S(1)} %copy.15, f32[352,1024]{1,0:T(8,128)} %get-tuple-element.666, bf16[352,1024]{1,0:T(8,128)(2,1)} %get-tuple-element.701, pred[]{:T(512)S(6)} %compare.5, f32[352]{0:T(512)S(1)} %convert_divide_fusion.3, s32[352]{0:T(512)S(1)} %get-tuple-element.635, ...), kind=kOutput, calls=%fused_computation.2.clone.1 | convolution fusion | flops 510214144 | bytes 4331017 | tf_op jit(solution)/shard_map/while/body/eval_jaxpr/mc,me->ce/dot_general | solution.py:122
  220.0 6.0 %collective-permute-done.1 = bf16[352,1024]{1,0:T(8,128)(2,1)S(1)} collective-permute-done((bf16[352,1024]{1,0:T(8,128)(2,1)}, bf16[352,1024]{1,0:T(8,128)(2,1)S(1)}, u32[]{:S(2)}, u32[]{:S(2)}) %collective-permute-start.1) | collective-permute-done | bytes 720928 | tf_op jit(solution)/shard_map/while/body/eval_jaxpr/ppermute | solution.py:12
  226.2 0.9 copy.16
  227.1 0.8 convert_divide_fusion.3
  227.9 0.8 dynamic-slice_add_fusion.4
  228.6 5.6 %convolution_add_fusion.8 = f32[352,1024]{1,0:T(8,128)} fusion(bf16[352,1024]{1,0:T(8,128)(2,1)} %copy.16, f32[352,1024]{1,0:T(8,128)} %get-tuple-element.665, bf16[352,1024]{1,0:T(8,128)(2,1)} %get-tuple-element.697, pred[]{:T(512)S(6)} %compare.5, f32[]{:T(128)} %get-tuple-element.698, f32[352]{0:T(512)S(1)} %divide_reduce_fusion.2, ...), kind=kOutput, calls=%fused_computation.3.clone.1 | convolution fusion | flops 510214144 | bytes 4331017 | tf_op jit(solution)/shard_map/while/body/eval_jaxpr/dot_general | solution.py:126
  234.2 5.3 %convolution_add_fusion.9 = f32[352,1024]{1,0:T(8,128)} fusion(bf16[352,1024]{1,0:T(8,128)(2,1)S(1)} %copy.15, f32[352,1024]{1,0:T(8,128)} %get-tuple-element.666, bf16[352,1024]{1,0:T(8,128)(2,1)} %get-tuple-element.701, pred[]{:T(512)S(6)} %compare.5, f32[352]{0:T(512)S(1)} %convert_divide_fusion.3, s32[352]{0:T(512)S(1)} %get-tuple-element.635, ...), kind=kOutput, calls=%fused_computation.2.clone.1 | convolution fusion | flops 510214144 | bytes 4331017 | tf_op jit(solution)/shard_map/while/body/eval_jaxpr/mc,me->ce/dot_general | solution.py:122
  239.5 6.0 %collective-permute-done.1 = bf16[352,1024]{1,0:T(8,128)(2,1)S(1)} collective-permute-done((bf16[352,1024]{1,0:T(8,128)(2,1)}, bf16[352,1024]{1,0:T(8,128)(2,1)S(1)}, u32[]{:S(2)}, u32[]{:S(2)}) %collective-permute-start.1) | collective-permute-done | bytes 720928 | tf_op jit(solution)/shard_map/while/body/eval_jaxpr/ppermute | solution.py:12
  245.5 4.3 %multiply_reduce_fusion.1 = (f32[352]{0:T(512)S(1)}, f32[352,1024]{1,0:T(8,128)}) fusion(f32[352,1024]{1,0:T(8,128)} %copy-done.3, f32[352]{0:T(512)S(1)} %add_rsqrt_fusion.1, f32[352,1024]{1,0:T(8,128)} %get-tuple-element.410, bf16[352,1024]{1,0:T(8,128)(2,1)S(1)} %get-tuple-element.411, bf16[352,1024]{1,0:T(8,128)(2,1)} %get-tuple-element.717, ...), kind=kOutput, calls=%fused_computation.72 | convolution fusion | flops 510934688 | bytes 5775624 | tf_op jit(solution)/shard_map/dot_general | solution.py:126
  249.8 2.2 fusion.110
  252.2 0.9 fusion.112
  254.0 1.9 fusion.56
  255.9 3.9 %multiply_reduce_fusion = (f32[352]{0:T(512)S(1)}, f32[352,1024]{1,0:T(8,128)}) fusion(f32[352,1024]{1,0:T(8,128)S(1)} %copy-done.2, f32[352]{0:T(512)S(1)} %add_rsqrt_fusion, f32[352,1024]{1,0:T(8,128)} %get-tuple-element.412, bf16[352,1024]{1,0:T(8,128)(2,1)S(1)} %get-tuple-element.413, bf16[352,1024]{1,0:T(8,128)(2,1)} %get-tuple-element.716, ...), kind=kOutput, calls=%fused_computation.69 | convolution fusion | flops 510934688 | bytes 5775624 | tf_op jit(solution)/shard_map/mc,me->ce/dot_general | solution.py:122
  259.8 1.8 fusion.111
  261.9 0.9 fusion.113
  263.2 1.9 fusion.57
  265.2 11.8 %reduce-scatter.2.cloned.1.call-done = bf16[352,256]{1,0:T(8,128)(2,1)} async-done(((bf16[352,1024]{1,0:T(8,128)(2,1)}), bf16[352,256]{1,0:T(8,128)(2,1)}) %reduce-scatter.2.cloned.1.call-update) | async-done | bytes 180240 | tf_op jit(solution)/shard_map/reduce_scatter | solution.py:145
  (89 shorter events, 5.2 us)
Async XLA Ops:
  7.2 51.4 %copy-start = (bf16[352,1024]{1,0:T(8,128)(2,1)S(1)}, bf16[352,1024]{1,0:T(8,128)(2,1)}, u32[]{:S(2)}) copy-start(bf16[352,1024]{1,0:T(8,128)(2,1)} %param.10) | copy-start | bytes 2162692
  7.2 51.4 %all-gather.5.cloned.1.call-start = ((), (), s32[]{:S(2)}) async-start(), calls=%async_computation.2 | async-start | bytes 2621440 | tf_op jit(solution)/shard_map/all_gather | solution.py:65
  7.9 96.7 %all-gather.3.cloned.1.call-start = ((), (), s32[]{:S(2)}) async-start(), calls=%async_computation.1 | async-start | bytes 2621440 | tf_op jit(solution)/shard_map/all_gather | solution.py:64
  8.7 268.3 %reduce-scatter.2.cloned.1.call-start = ((), (), s32[]{:S(2)}) async-start(), calls=%async_computation.3 | async-start | bytes 901120 | tf_op jit(solution)/shard_map/reduce_scatter | solution.py:145
  13.8 90.8 %copy-start.11 = (bf16[352,1024]{1,0:T(8,128)(2,1)S(1)}, bf16[352,1024]{1,0:T(8,128)(2,1)}, u32[]{:S(2)}) copy-start(bf16[352,1024]{1,0:T(8,128)(2,1)} %param.9) | copy-start | bytes 2162692
  61.2 46.1 %copy-start.1 = (f32[352,1024]{1,0:T(8,128)}, f32[352,1024]{1,0:T(8,128)S(1)}, u32[]{:S(2)}) copy-start(f32[352,1024]{1,0:T(8,128)S(1)} %get-tuple-element.522) | copy-start | bytes 4325380
  107.2 1.1 copy-start.3
  108.3 0.8 copy-start.7
  108.3 1.1 copy-start.8
  109.5 14.0 %collective-permute-start = (bf16[352,1024]{1,0:T(8,128)(2,1)S(1)}, bf16[352,1024]{1,0:T(8,128)(2,1)S(1)}, u32[]{:S(2)}, u32[]{:S(2)}) collective-permute-start(bf16[352,1024]{1,0:T(8,128)(2,1)S(1)} %copy.15), channel_id=1, source_target_pairs={{0,4},{4,8},{8,12},{12,16},{16,20},{20,24},{24,28},{28,0},{1,5},{5... | collective-permute-start | bytes 2162696 | tf_op jit(solution)/shard_map/while/body/eval_jaxpr/ppermute | solution.py:12
  110.4 18.5 %collective-permute-start.1 = (bf16[352,1024]{1,0:T(8,128)(2,1)}, bf16[352,1024]{1,0:T(8,128)(2,1)S(1)}, u32[]{:S(2)}, u32[]{:S(2)}) collective-permute-start(bf16[352,1024]{1,0:T(8,128)(2,1)} %copy.16), channel_id=1, source_target_pairs={{0,4},{4,8},{8,12},{12,16},{16,20},{20,24},{24,28},{28,0},{1,5},{5... | collective-permute-start | bytes 2162696 | tf_op jit(solution)/shard_map/while/body/eval_jaxpr/ppermute | solution.py:12
  128.9 14.0 %collective-permute-start = (bf16[352,1024]{1,0:T(8,128)(2,1)S(1)}, bf16[352,1024]{1,0:T(8,128)(2,1)S(1)}, u32[]{:S(2)}, u32[]{:S(2)}) collective-permute-start(bf16[352,1024]{1,0:T(8,128)(2,1)S(1)} %copy.15), channel_id=1, source_target_pairs={{0,4},{4,8},{8,12},{12,16},{16,20},{20,24},{24,28},{28,0},{1,5},{5... | collective-permute-start | bytes 2162696 | tf_op jit(solution)/shard_map/while/body/eval_jaxpr/ppermute | solution.py:12
  129.8 18.5 %collective-permute-start.1 = (bf16[352,1024]{1,0:T(8,128)(2,1)}, bf16[352,1024]{1,0:T(8,128)(2,1)S(1)}, u32[]{:S(2)}, u32[]{:S(2)}) collective-permute-start(bf16[352,1024]{1,0:T(8,128)(2,1)} %copy.16), channel_id=1, source_target_pairs={{0,4},{4,8},{8,12},{12,16},{16,20},{20,24},{24,28},{28,0},{1,5},{5... | collective-permute-start | bytes 2162696 | tf_op jit(solution)/shard_map/while/body/eval_jaxpr/ppermute | solution.py:12
  148.3 13.4 %collective-permute-start = (bf16[352,1024]{1,0:T(8,128)(2,1)S(1)}, bf16[352,1024]{1,0:T(8,128)(2,1)S(1)}, u32[]{:S(2)}, u32[]{:S(2)}) collective-permute-start(bf16[352,1024]{1,0:T(8,128)(2,1)S(1)} %copy.15), channel_id=1, source_target_pairs={{0,4},{4,8},{8,12},{12,16},{16,20},{20,24},{24,28},{28,0},{1,5},{5... | collective-permute-start | bytes 2162696 | tf_op jit(solution)/shard_map/while/body/eval_jaxpr/ppermute | solution.py:12
  149.3 18.5 %collective-permute-start.1 = (bf16[352,1024]{1,0:T(8,128)(2,1)}, bf16[352,1024]{1,0:T(8,128)(2,1)S(1)}, u32[]{:S(2)}, u32[]{:S(2)}) collective-permute-start(bf16[352,1024]{1,0:T(8,128)(2,1)} %copy.16), channel_id=1, source_target_pairs={{0,4},{4,8},{8,12},{12,16},{16,20},{20,24},{24,28},{28,0},{1,5},{5... | collective-permute-start | bytes 2162696 | tf_op jit(solution)/shard_map/while/body/eval_jaxpr/ppermute | solution.py:12
  167.8 13.4 %collective-permute-start = (bf16[352,1024]{1,0:T(8,128)(2,1)S(1)}, bf16[352,1024]{1,0:T(8,128)(2,1)S(1)}, u32[]{:S(2)}, u32[]{:S(2)}) collective-permute-start(bf16[352,1024]{1,0:T(8,128)(2,1)S(1)} %copy.15), channel_id=1, source_target_pairs={{0,4},{4,8},{8,12},{12,16},{16,20},{20,24},{24,28},{28,0},{1,5},{5... | collective-permute-start | bytes 2162696 | tf_op jit(solution)/shard_map/while/body/eval_jaxpr/ppermute | solution.py:12
  168.7 18.5 %collective-permute-start.1 = (bf16[352,1024]{1,0:T(8,128)(2,1)}, bf16[352,1024]{1,0:T(8,128)(2,1)S(1)}, u32[]{:S(2)}, u32[]{:S(2)}) collective-permute-start(bf16[352,1024]{1,0:T(8,128)(2,1)} %copy.16), channel_id=1, source_target_pairs={{0,4},{4,8},{8,12},{12,16},{16,20},{20,24},{24,28},{28,0},{1,5},{5... | collective-permute-start | bytes 2162696 | tf_op jit(solution)/shard_map/while/body/eval_jaxpr/ppermute | solution.py:12
  187.2 13.4 %collective-permute-start = (bf16[352,1024]{1,0:T(8,128)(2,1)S(1)}, bf16[352,1024]{1,0:T(8,128)(2,1)S(1)}, u32[]{:S(2)}, u32[]{:S(2)}) collective-permute-start(bf16[352,1024]{1,0:T(8,128)(2,1)S(1)} %copy.15), channel_id=1, source_target_pairs={{0,4},{4,8},{8,12},{12,16},{16,20},{20,24},{24,28},{28,0},{1,5},{5... | collective-permute-start | bytes 2162696 | tf_op jit(solution)/shard_map/while/body/eval_jaxpr/ppermute | solution.py:12
  188.1 18.5 %collective-permute-start.1 = (bf16[352,1024]{1,0:T(8,128)(2,1)}, bf16[352,1024]{1,0:T(8,128)(2,1)S(1)}, u32[]{:S(2)}, u32[]{:S(2)}) collective-permute-start(bf16[352,1024]{1,0:T(8,128)(2,1)} %copy.16), channel_id=1, source_target_pairs={{0,4},{4,8},{8,12},{12,16},{16,20},{20,24},{24,28},{28,0},{1,5},{5... | collective-permute-start | bytes 2162696 | tf_op jit(solution)/shard_map/while/body/eval_jaxpr/ppermute | solution.py:12
  206.7 13.4 %collective-permute-start = (bf16[352,1024]{1,0:T(8,128)(2,1)S(1)}, bf16[352,1024]{1,0:T(8,128)(2,1)S(1)}, u32[]{:S(2)}, u32[]{:S(2)}) collective-permute-start(bf16[352,1024]{1,0:T(8,128)(2,1)S(1)} %copy.15), channel_id=1, source_target_pairs={{0,4},{4,8},{8,12},{12,16},{16,20},{20,24},{24,28},{28,0},{1,5},{5... | collective-permute-start | bytes 2162696 | tf_op jit(solution)/shard_map/while/body/eval_jaxpr/ppermute | solution.py:12
  207.6 18.5 %collective-permute-start.1 = (bf16[352,1024]{1,0:T(8,128)(2,1)}, bf16[352,1024]{1,0:T(8,128)(2,1)S(1)}, u32[]{:S(2)}, u32[]{:S(2)}) collective-permute-start(bf16[352,1024]{1,0:T(8,128)(2,1)} %copy.16), channel_id=1, source_target_pairs={{0,4},{4,8},{8,12},{12,16},{16,20},{20,24},{24,28},{28,0},{1,5},{5... | collective-permute-start | bytes 2162696 | tf_op jit(solution)/shard_map/while/body/eval_jaxpr/ppermute | solution.py:12
  226.1 13.4 %collective-permute-start = (bf16[352,1024]{1,0:T(8,128)(2,1)S(1)}, bf16[352,1024]{1,0:T(8,128)(2,1)S(1)}, u32[]{:S(2)}, u32[]{:S(2)}) collective-permute-start(bf16[352,1024]{1,0:T(8,128)(2,1)S(1)} %copy.15), channel_id=1, source_target_pairs={{0,4},{4,8},{8,12},{12,16},{16,20},{20,24},{24,28},{28,0},{1,5},{5... | collective-permute-start | bytes 2162696 | tf_op jit(solution)/shard_map/while/body/eval_jaxpr/ppermute | solution.py:12
  227.0 18.5 %collective-permute-start.1 = (bf16[352,1024]{1,0:T(8,128)(2,1)}, bf16[352,1024]{1,0:T(8,128)(2,1)S(1)}, u32[]{:S(2)}, u32[]{:S(2)}) collective-permute-start(bf16[352,1024]{1,0:T(8,128)(2,1)} %copy.16), channel_id=1, source_target_pairs={{0,4},{4,8},{8,12},{12,16},{16,20},{20,24},{24,28},{28,0},{1,5},{5... | collective-permute-start | bytes 2162696 | tf_op jit(solution)/shard_map/while/body/eval_jaxpr/ppermute | solution.py:12
  249.8 2.5 copy-start.10
  252.2 1.4 copy-start.4
  252.2 1.8 copy-start.6
  254.0 1.9 copy-start.2
  259.8 2.0 copy-start.9
  261.9 1.4 copy-start.5
Sparse Core Ops, SparseCore 0:
  9.5 48.9 all-gather.4
  60.1 44.4 all-gather.2
  256.0 20.9 reduce-scatter.1
where the time goes:
time: 285 us; the launch traced here: 284 us
  waiting for transfers between devices  142 us (50%)
  matrix products  94 us (33%)
  other arithmetic  19 us (7%)
  between operations  15.2 us (5%)
  local copies, waits for them, and re-layouts  10.2 us (4%)
    all_gather x1, waiting for transfers between devices, body(): lax.all_gather(sentence_projector_matrix, 'tensor', axis=1, tiled=True)  44.7 us
    all_gather x1, waiting for transfers between devices, body(): lax.all_gather(picture_projector_matrix, 'tensor', axis=1, tiled=True)  43.4 us
    dot_general x8, matrix products, pair_work(): jnp.dot(coef_b, cap_block, preferred_element_type=jnp.float32)  42.9 us
    ppermute x14, waiting for transfers between devices, passed_along(): return lax.ppermute(value, axis, pairs)  40.8 us
    dot_general x8, matrix products, pair_work(): jnp.einsum('mc,me->ce', coef_a, img_block, preferred_element_type=jnp.flo...  40.2 us
    reduce_scatter x1, waiting for transfers between devices, body(): lax.psum_scatter(img_part.astype(jnp.bfloat16), 'tensor', scatter_dimensi...  11.8 us
    div x15, other arithmetic, scaling_factor(): 1.0 / sentence_tally_later.astype(jnp.float32)  6.45 us
    while x14, local copies, waits for them, and re-layouts  6.33 us
  transfers between devices with their start and end apart: 17, of which 10 were waited for; matrix products, arithmetic and copies ran while one was open for 38% of the time, Pallas kernels for 0%

commit v1 on v0

--- a/solution.py
+++ b/solution.py
@@ -4,6 +4,27 @@
 from jax.sharding import PartitionSpec as P
 
 epsilon = 1e-06
+
+
+def ring_gather(value, axis, dim):
+    size, index, rows = (lax.axis_size(axis), lax.axis_index(axis), value.shape[dim])
+    upward = [(i, (i + 1) % size) for i in range(size)]
+    left = [(i, (i - 1) % size) for i in range(size)]
+    filled = jnp.zeros((*value.shape[:dim], size * rows, *value.shape[dim + 1 :]), value.dtype)
+    filled = lax.dynamic_update_slice_in_dim(filled, value, index * rows, axis=dim)
+    from_left = from_right = value
+    half = size // 2
+    for step in range(1, half + 1):
+        from_left = lax.ppermute(from_left, axis, upward)
+        filled = lax.dynamic_update_slice_in_dim(
+            filled, from_left, (index - step) % size * rows, axis=dim
+        )
+        if step < size - half:
+            from_right = lax.ppermute(from_right, axis, left)
+            filled = lax.dynamic_update_slice_in_dim(
+                filled, from_right, (index + step) % size * rows, axis=dim
+            )
+    return filled
 
 
 def passed_along(value, axis, steps):
@@ -62,7 +83,7 @@
 ):
     full_img, full_cap = (
         lax.all_gather(picture_projector_matrix, "tensor", axis=1, tiled=True),
-        lax.all_gather(sentence_projector_matrix, "tensor", axis=1, tiled=True),
+        ring_gather(sentence_projector_matrix, "tensor", 1),
     )
     img_unit, img_scale = embed(picture_encoder_result, full_img)
     cap_unit, cap_scale = embed(sentence_encoder_result, full_cap)

time: 285 us -> 262 us (0.919)
  waiting for transfers between devices: 142 us -> 100 us
  starting transfers between devices: 2.77 us -> 20.6 us
    all_gather x1 -> x0, waiting for transfers between devices: 44.7 us -> none  [body(): lax.all_gather(sentence_projector_matrix, 'tensor', axis=1, tiled=True)]
    ppermute x0 -> x3, waiting for transfers between devices: none -> 39.1 us  [the longest x2 21.4 us: ring_gather(): from_left = lax.ppermute(from_left, axis, upward)]
    all_gather x1, waiting for transfers between devices: 43.4 us -> 7.85 us  [body(): lax.all_gather(picture_projector_matrix, 'tensor', axis=1, tiled=True)]
    ppermute x0 -> x3, starting transfers between devices: none -> 17.7 us  [the longest x2 15.6 us: ring_gather(): from_left = lax.ppermute(from_left, axis, upward)]
  transfers between devices with their start and end apart: 17 -> 19, of which waited for: 10 -> 12; matrix products, arithmetic and copies ran while one was open for 38% -> 41% of each run, Pallas kernels for 0% -> 0%
where the time goes in v1:
time: 262 us; the launch traced here: 261 us
  waiting for transfers between devices  100 us (38%)
  matrix products  92.6 us (35%)
  starting transfers between devices  20.6 us (8%)
  other arithmetic  19.1 us (7%)
  between operations  15.6 us (6%)
  local copies, waits for them, and re-layouts  12.4 us (5%)
    dot_general x8, matrix products, pair_work(): jnp.dot(coef_b, cap_block, preferred_element_type=jnp.float32)  43.2 us
    ppermute x14, waiting for transfers between devices, passed_along(): return lax.ppermute(value, axis, pairs)  40.6 us
    dot_general x8, matrix products, pair_work(): jnp.einsum('mc,me->ce', coef_a, img_block, preferred_element_type=jnp.flo...  40.1 us
    ppermute x2, waiting for transfers between devices, ring_gather(): from_left = lax.ppermute(from_left, axis, upward)  21.4 us
    ppermute x1, waiting for transfers between devices, ring_gather(): from_right = lax.ppermute(from_right, axis, left)  17.7 us
    ppermute x2, starting transfers between devices, ring_gather(): from_left = lax.ppermute(from_left, axis, upward)  15.6 us
    reduce_scatter x1, waiting for transfers between devices, body(): lax.psum_scatter(img_part.astype(jnp.bfloat16), 'tensor', scatter_dimensi...  12.3 us
    all_gather x1, waiting for transfers between devices, body(): lax.all_gather(picture_projector_matrix, 'tensor', axis=1, tiled=True)  7.85 us
  transfers between devices with their start and end apart: 19, of which 12 were waited for; matrix products, arithmetic and copies ran while one was open for 41% of the time, Pallas kernels for 0%

profile of v1, /device:TPU:0, one launch (start us, length us, event | category | flops | bytes accessed | tf_op | source)
XLA Modules:
  0.0 260.8 jit_solution(12873240689432434047)
XLA Ops:
  8.0 3.1 %collective-permute-start.2 = (bf16[1024,256]{1,0:T(8,128)(2,1)}, bf16[1024,256]{1,0:T(8,128)(2,1)S(1)}, u32[]{:S(2)}, u32[]{:S(2)}) collective-permute-start(bf16[1024,256]{1,0:T(8,128)(2,1)} %param.12), channel_id=1, source_target_pairs={{0,1},{1,2},{2,3},{3,0},{4,5},{5,6},{6,7},{7,4},{8,9},{9,10},{10,1... | collective-permute-start | bytes 1572872 | tf_op jit(solution)/shard_map/ppermute | solution.py:18
  11.1 2.1 collective-permute-start.3
  13.2 1.0 reduce-window.9
  14.4 0.8 bitcast_subtract_fusion
  15.2 0.9 dynamic-slice_add_fusion.1
  16.0 0.8 broadcast_divide_fusion
  16.9 10.8 %collective-permute-done.2 = bf16[1024,256]{1,0:T(8,128)(2,1)S(1)} collective-permute-done((bf16[1024,256]{1,0:T(8,128)(2,1)}, bf16[1024,256]{1,0:T(8,128)(2,1)S(1)}, u32[]{:S(2)}, u32[]{:S(2)}) %collective-permute-start.2) | collective-permute-done | bytes 524320 | tf_op jit(solution)/shard_map/ppermute | solution.py:18
  27.7 12.5 %collective-permute-start.4 = (bf16[1024,256]{1,0:T(8,128)(2,1)S(1)}, bf16[1024,256]{1,0:T(8,128)(2,1)S(1)}, u32[]{:S(2)}, u32[]{:S(2)}) collective-permute-start(bf16[1024,256]{1,0:T(8,128)(2,1)S(1)} %collective-permute-done.2), channel_id=1, source_target_pairs={{0,1},{1,2},{2,3},{3,0},{4,5},{5,6},{6,7},{7,4},{8,9},{9,10},{10,1... | collective-permute-start | bytes 1572872 | tf_op jit(solution)/shard_map/ppermute | solution.py:18
  41.9 17.7 %collective-permute-done.3 = bf16[1024,256]{1,0:T(8,128)(2,1)S(1)} collective-permute-done((bf16[1024,256]{1,0:T(8,128)(2,1)}, bf16[1024,256]{1,0:T(8,128)(2,1)S(1)}, u32[]{:S(2)}, u32[]{:S(2)}) %collective-permute-start.3) | collective-permute-done | bytes 524320 | tf_op jit(solution)/shard_map/ppermute | solution.py:23
  59.7 10.6 %collective-permute-done.4 = bf16[1024,256]{1,0:T(8,128)(2,1)S(1)} collective-permute-done((bf16[1024,256]{1,0:T(8,128)(2,1)S(1)}, bf16[1024,256]{1,0:T(8,128)(2,1)S(1)}, u32[]{:S(2)}, u32[]{:S(2)}) %collective-permute-start.4) | collective-permute-done | bytes 524320 | tf_op jit(solution)/shard_map/ppermute | solution.py:18
  70.4 1.0 multiply_reduce_fusion.1
  71.7 1.1 copy-done.3
  73.0 0.9 copy-done.9
  73.9 7.8 %all-gather.2.cloned.1.call-done = bf16[1024,1024]{1,0:T(8,128)(2,1)} async-done(((bf16[1024,256]{1,0:T(8,128)(2,1)}), bf16[1024,1024]{1,0:T(8,128)(2,1)}) %all-gather.2.cloned.1.call-update) | async-done | bytes 2097168 | tf_op jit(solution)/shard_map/all_gather | solution.py:85
  81.7 2.6 multiply_reduce_fusion.2
  84.6 0.9 copy-done.1
  85.7 136.1 %while.22 = (s32[]{:T(128)}, bf16[352,1024]{1,0:T(8,128)(2,1)S(1)}, bf16[352,1024]{1,0:T(8,128)(2,1)S(1)}, f32[352,1024]{1,0:T(8,128)}, f32[352,1024]{1,0:T(8,12...) while((s32[]{:T(128)}, bf16[352,1024]{1,0:T(8,128)(2,1)S(1)}, ...), condition=%wide.region_5.6_spmd.clone, body=%wide.region_4.5_spmd.clone.sunk | while | flops 1020430464 | bytes 17330208 | solution.py:162
  85.8 0.9 copy.20
  86.7 1.6 collective-permute-start.1
  88.4 0.8 convert_divide_fusion.3
  89.1 0.8 dynamic-slice_add_fusion.4
  89.9 5.2 %convolution_add_fusion.8 = f32[352,1024]{1,0:T(8,128)} fusion(bf16[352,1024]{1,0:T(8,128)(2,1)} %copy.20, f32[352,1024]{1,0:T(8,128)} %get-tuple-element.663, bf16[352,1024]{1,0:T(8,128)(2,1)} %get-tuple-element.695, pred[]{:T(512)S(6)} %compare.8, f32[]{:T(128)} %get-tuple-element.696, f32[352]{0:T(512)S(1)} %divide_reduce_fusion.2, ...), kind=kOutput, calls=%fused_computation.3.clone.1 | convolution fusion | flops 510214144 | bytes 4331017 | tf_op jit(solution)/shard_map/while/body/eval_jaxpr/dot_general | solution.py:147
  95.1 4.8 %convolution_add_fusion.9 = f32[352,1024]{1,0:T(8,128)} fusion(bf16[352,1024]{1,0:T(8,128)(2,1)S(1)} %copy.19, f32[352,1024]{1,0:T(8,128)} %get-tuple-element.664, bf16[352,1024]{1,0:T(8,128)(2,1)} %get-tuple-element.699, pred[]{:T(512)S(6)} %compare.8, f32[352]{0:T(512)S(1)} %convert_divide_fusion.3, s32[352]{0:T(512)S(1)} %get-tuple-element.633, ...), kind=kOutput, calls=%fused_computation.2.clone.1 | convolution fusion | flops 510214144 | bytes 4331017 | tf_op jit(solution)/shard_map/while/body/eval_jaxpr/mc,me->ce/dot_general | solution.py:143
  99.8 5.3 %collective-permute-done.1 = bf16[352,1024]{1,0:T(8,128)(2,1)S(1)} collective-permute-done((bf16[352,1024]{1,0:T(8,128)(2,1)}, bf16[352,1024]{1,0:T(8,128)(2,1)S(1)}, u32[]{:S(2)}, u32[]{:S(2)}) %collective-permute-start.1) | collective-permute-done | bytes 720928 | tf_op jit(solution)/shard_map/while/body/eval_jaxpr/ppermute | solution.py:33
  105.2 0.9 copy.20
  108.4 5.6 %convolution_add_fusion.8 = f32[352,1024]{1,0:T(8,128)} fusion(bf16[352,1024]{1,0:T(8,128)(2,1)} %copy.20, f32[352,1024]{1,0:T(8,128)} %get-tuple-element.663, bf16[352,1024]{1,0:T(8,128)(2,1)} %get-tuple-element.695, pred[]{:T(512)S(6)} %compare.8, f32[]{:T(128)} %get-tuple-element.696, f32[352]{0:T(512)S(1)} %divide_reduce_fusion.2, ...), kind=kOutput, calls=%fused_computation.3.clone.1 | convolution fusion | flops 510214144 | bytes 4331017 | tf_op jit(solution)/shard_map/while/body/eval_jaxpr/dot_general | solution.py:147
  114.0 5.3 %convolution_add_fusion.9 = f32[352,1024]{1,0:T(8,128)} fusion(bf16[352,1024]{1,0:T(8,128)(2,1)S(1)} %copy.19, f32[352,1024]{1,0:T(8,128)} %get-tuple-element.664, bf16[352,1024]{1,0:T(8,128)(2,1)} %get-tuple-element.699, pred[]{:T(512)S(6)} %compare.8, f32[352]{0:T(512)S(1)} %convert_divide_fusion.3, s32[352]{0:T(512)S(1)} %get-tuple-element.633, ...), kind=kOutput, calls=%fused_computation.2.clone.1 | convolution fusion | flops 510214144 | bytes 4331017 | tf_op jit(solution)/shard_map/while/body/eval_jaxpr/mc,me->ce/dot_general | solution.py:143
  119.3 5.3 %collective-permute-done.1 = bf16[352,1024]{1,0:T(8,128)(2,1)S(1)} collective-permute-done((bf16[352,1024]{1,0:T(8,128)(2,1)}, bf16[352,1024]{1,0:T(8,128)(2,1)S(1)}, u32[]{:S(2)}, u32[]{:S(2)}) %collective-permute-start.1) | collective-permute-done | bytes 720928 | tf_op jit(solution)/shard_map/while/body/eval_jaxpr/ppermute | solution.py:33
  124.7 0.9 copy.20
  127.1 5.6 %convolution_add_fusion.8 = f32[352,1024]{1,0:T(8,128)} fusion(bf16[352,1024]{1,0:T(8,128)(2,1)} %copy.20, f32[352,1024]{1,0:T(8,128)} %get-tuple-element.663, bf16[352,1024]{1,0:T(8,128)(2,1)} %get-tuple-element.695, pred[]{:T(512)S(6)} %compare.8, f32[]{:T(128)} %get-tuple-element.696, f32[352]{0:T(512)S(1)} %divide_reduce_fusion.2, ...), kind=kOutput, calls=%fused_computation.3.clone.1 | convolution fusion | flops 510214144 | bytes 4331017 | tf_op jit(solution)/shard_map/while/body/eval_jaxpr/dot_general | solution.py:147
  132.7 5.3 %convolution_add_fusion.9 = f32[352,1024]{1,0:T(8,128)} fusion(bf16[352,1024]{1,0:T(8,128)(2,1)S(1)} %copy.19, f32[352,1024]{1,0:T(8,128)} %get-tuple-element.664, bf16[352,1024]{1,0:T(8,128)(2,1)} %get-tuple-element.699, pred[]{:T(512)S(6)} %compare.8, f32[352]{0:T(512)S(1)} %convert_divide_fusion.3, s32[352]{0:T(512)S(1)} %get-tuple-element.633, ...), kind=kOutput, calls=%fused_computation.2.clone.1 | convolution fusion | flops 510214144 | bytes 4331017 | tf_op jit(solution)/shard_map/while/body/eval_jaxpr/mc,me->ce/dot_general | solution.py:143
  138.0 6.0 %collective-permute-done.1 = bf16[352,1024]{1,0:T(8,128)(2,1)S(1)} collective-permute-done((bf16[352,1024]{1,0:T(8,128)(2,1)}, bf16[352,1024]{1,0:T(8,128)(2,1)S(1)}, u32[]{:S(2)}, u32[]{:S(2)}) %collective-permute-start.1) | collective-permute-done | bytes 720928 | tf_op jit(solution)/shard_map/while/body/eval_jaxpr/ppermute | solution.py:33
  144.1 0.9 copy.20
  145.0 0.8 convert_divide_fusion.3
  145.8 0.8 dynamic-slice_add_fusion.4
  146.6 5.6 %convolution_add_fusion.8 = f32[352,1024]{1,0:T(8,128)} fusion(bf16[352,1024]{1,0:T(8,128)(2,1)} %copy.20, f32[352,1024]{1,0:T(8,128)} %get-tuple-element.663, bf16[352,1024]{1,0:T(8,128)(2,1)} %get-tuple-element.695, pred[]{:T(512)S(6)} %compare.8, f32[]{:T(128)} %get-tuple-element.696, f32[352]{0:T(512)S(1)} %divide_reduce_fusion.2, ...), kind=kOutput, calls=%fused_computation.3.clone.1 | convolution fusion | flops 510214144 | bytes 4331017 | tf_op jit(solution)/shard_map/while/body/eval_jaxpr/dot_general | solution.py:147
  152.2 5.3 %convolution_add_fusion.9 = f32[352,1024]{1,0:T(8,128)} fusion(bf16[352,1024]{1,0:T(8,128)(2,1)S(1)} %copy.19, f32[352,1024]{1,0:T(8,128)} %get-tuple-element.664, bf16[352,1024]{1,0:T(8,128)(2,1)} %get-tuple-element.699, pred[]{:T(512)S(6)} %compare.8, f32[352]{0:T(512)S(1)} %convert_divide_fusion.3, s32[352]{0:T(512)S(1)} %get-tuple-element.633, ...), kind=kOutput, calls=%fused_computation.2.clone.1 | convolution fusion | flops 510214144 | bytes 4331017 | tf_op jit(solution)/shard_map/while/body/eval_jaxpr/mc,me->ce/dot_general | solution.py:143
  157.4 6.0 %collective-permute-done.1 = bf16[352,1024]{1,0:T(8,128)(2,1)S(1)} collective-permute-done((bf16[352,1024]{1,0:T(8,128)(2,1)}, bf16[352,1024]{1,0:T(8,128)(2,1)S(1)}, u32[]{:S(2)}, u32[]{:S(2)}) %collective-permute-start.1) | collective-permute-done | bytes 720928 | tf_op jit(solution)/shard_map/while/body/eval_jaxpr/ppermute | solution.py:33
  163.6 0.9 copy.20
  164.5 0.8 convert_divide_fusion.3
  165.3 0.8 dynamic-slice_add_fusion.4
  166.0 5.6 %convolution_add_fusion.8 = f32[352,1024]{1,0:T(8,128)} fusion(bf16[352,1024]{1,0:T(8,128)(2,1)} %copy.20, f32[352,1024]{1,0:T(8,128)} %get-tuple-element.663, bf16[352,1024]{1,0:T(8,128)(2,1)} %get-tuple-element.695, pred[]{:T(512)S(6)} %compare.8, f32[]{:T(128)} %get-tuple-element.696, f32[352]{0:T(512)S(1)} %divide_reduce_fusion.2, ...), kind=kOutput, calls=%fused_computation.3.clone.1 | convolution fusion | flops 510214144 | bytes 4331017 | tf_op jit(solution)/shard_map/while/body/eval_jaxpr/dot_general | solution.py:147
  171.6 5.3 %convolution_add_fusion.9 = f32[352,1024]{1,0:T(8,128)} fusion(bf16[352,1024]{1,0:T(8,128)(2,1)S(1)} %copy.19, f32[352,1024]{1,0:T(8,128)} %get-tuple-element.664, bf16[352,1024]{1,0:T(8,128)(2,1)} %get-tuple-element.699, pred[]{:T(512)S(6)} %compare.8, f32[352]{0:T(512)S(1)} %convert_divide_fusion.3, s32[352]{0:T(512)S(1)} %get-tuple-element.633, ...), kind=kOutput, calls=%fused_computation.2.clone.1 | convolution fusion | flops 510214144 | bytes 4331017 | tf_op jit(solution)/shard_map/while/body/eval_jaxpr/mc,me->ce/dot_general | solution.py:143
  176.9 6.0 %collective-permute-done.1 = bf16[352,1024]{1,0:T(8,128)(2,1)S(1)} collective-permute-done((bf16[352,1024]{1,0:T(8,128)(2,1)}, bf16[352,1024]{1,0:T(8,128)(2,1)S(1)}, u32[]{:S(2)}, u32[]{:S(2)}) %collective-permute-start.1) | collective-permute-done | bytes 720928 | tf_op jit(solution)/shard_map/while/body/eval_jaxpr/ppermute | solution.py:33
  183.0 0.9 copy.20
  183.9 0.8 convert_divide_fusion.3
  184.7 0.8 dynamic-slice_add_fusion.4
  185.5 5.6 %convolution_add_fusion.8 = f32[352,1024]{1,0:T(8,128)} fusion(bf16[352,1024]{1,0:T(8,128)(2,1)} %copy.20, f32[352,1024]{1,0:T(8,128)} %get-tuple-element.663, bf16[352,1024]{1,0:T(8,128)(2,1)} %get-tuple-element.695, pred[]{:T(512)S(6)} %compare.8, f32[]{:T(128)} %get-tuple-element.696, f32[352]{0:T(512)S(1)} %divide_reduce_fusion.2, ...), kind=kOutput, calls=%fused_computation.3.clone.1 | convolution fusion | flops 510214144 | bytes 4331017 | tf_op jit(solution)/shard_map/while/body/eval_jaxpr/dot_general | solution.py:147
  191.1 5.3 %convolution_add_fusion.9 = f32[352,1024]{1,0:T(8,128)} fusion(bf16[352,1024]{1,0:T(8,128)(2,1)S(1)} %copy.19, f32[352,1024]{1,0:T(8,128)} %get-tuple-element.664, bf16[352,1024]{1,0:T(8,128)(2,1)} %get-tuple-element.699, pred[]{:T(512)S(6)} %compare.8, f32[352]{0:T(512)S(1)} %convert_divide_fusion.3, s32[352]{0:T(512)S(1)} %get-tuple-element.633, ...), kind=kOutput, calls=%fused_computation.2.clone.1 | convolution fusion | flops 510214144 | bytes 4331017 | tf_op jit(solution)/shard_map/while/body/eval_jaxpr/mc,me->ce/dot_general | solution.py:143
  196.3 6.0 %collective-permute-done.1 = bf16[352,1024]{1,0:T(8,128)(2,1)S(1)} collective-permute-done((bf16[352,1024]{1,0:T(8,128)(2,1)}, bf16[352,1024]{1,0:T(8,128)(2,1)S(1)}, u32[]{:S(2)}, u32[]{:S(2)}) %collective-permute-start.1) | collective-permute-done | bytes 720928 | tf_op jit(solution)/shard_map/while/body/eval_jaxpr/ppermute | solution.py:33
  202.4 0.9 copy.20
  203.4 0.8 convert_divide_fusion.3
  204.9 5.6 %convolution_add_fusion.8 = f32[352,1024]{1,0:T(8,128)} fusion(bf16[352,1024]{1,0:T(8,128)(2,1)} %copy.20, f32[352,1024]{1,0:T(8,128)} %get-tuple-element.663, bf16[352,1024]{1,0:T(8,128)(2,1)} %get-tuple-element.695, pred[]{:T(512)S(6)} %compare.8, f32[]{:T(128)} %get-tuple-element.696, f32[352]{0:T(512)S(1)} %divide_reduce_fusion.2, ...), kind=kOutput, calls=%fused_computation.3.clone.1 | convolution fusion | flops 510214144 | bytes 4331017 | tf_op jit(solution)/shard_map/while/body/eval_jaxpr/dot_general | solution.py:147
  210.5 5.3 %convolution_add_fusion.9 = f32[352,1024]{1,0:T(8,128)} fusion(bf16[352,1024]{1,0:T(8,128)(2,1)S(1)} %copy.19, f32[352,1024]{1,0:T(8,128)} %get-tuple-element.664, bf16[352,1024]{1,0:T(8,128)(2,1)} %get-tuple-element.699, pred[]{:T(512)S(6)} %compare.8, f32[352]{0:T(512)S(1)} %convert_divide_fusion.3, s32[352]{0:T(512)S(1)} %get-tuple-element.633, ...), kind=kOutput, calls=%fused_computation.2.clone.1 | convolution fusion | flops 510214144 | bytes 4331017 | tf_op jit(solution)/shard_map/while/body/eval_jaxpr/mc,me->ce/dot_general | solution.py:143
  215.8 6.0 %collective-permute-done.1 = bf16[352,1024]{1,0:T(8,128)(2,1)S(1)} collective-permute-done((bf16[352,1024]{1,0:T(8,128)(2,1)}, bf16[352,1024]{1,0:T(8,128)(2,1)S(1)}, u32[]{:S(2)}, u32[]{:S(2)}) %collective-permute-start.1) | collective-permute-done | bytes 720928 | tf_op jit(solution)/shard_map/while/body/eval_jaxpr/ppermute | solution.py:33
  221.8 4.5 %multiply_reduce_fusion = (f32[352]{0:T(512)S(1)}, f32[352,1024]{1,0:T(8,128)}) fusion(f32[352,1024]{1,0:T(8,128)} %copy-done.1, f32[352]{0:T(512)S(1)} %add_rsqrt_fusion.1, f32[352,1024]{1,0:T(8,128)} %get-tuple-element.410, bf16[352,1024]{1,0:T(8,128)(2,1)S(1)} %get-tuple-element.411, f32[]{:T(128)} %bitcast.56, f32[352]{0:T(512)S(1)} %get-tuple-element.511, ...), kind=kOutput, calls=%fused_computation.76 | convolution fusion | flops 511655584 | bytes 5054728 | tf_op jit(solution)/shard_map/dot_general | solution.py:147
  226.3 2.2 fusion.114
  228.8 0.9 fusion.117
  230.6 1.9 fusion.59
  232.5 3.8 %fusion.56 = (f32[352]{0:T(512)S(1)}, f32[352,1024]{1,0:T(8,128)}) fusion(f32[1024,352]{0,1:T(8,128)S(1)} %copy-done.4, f32[352]{0:T(512)S(1)} %add_rsqrt_fusion, f32[352,1024]{1,0:T(8,128)} %get-tuple-element.412, bf16[352,1024]{1,0:T(8,128)(2,1)S(1)} %get-tuple-element.413, f32[352]{0:T(512)S(1)} %get-tuple-element.518, s32[352]{0:T(512)S(1)} %iota_add_fusion.3, ...), kind=kOutput, calls=%fused_computation.70 | convolution fusion | flops 511655584 | bytes 5054728 | tf_op jit(solution)/shard_map/mc,me->ce/dot_general | solution.py:143
  236.3 1.8 fusion.116
  238.8 1.1 fusion.79
  239.9 1.8 fusion.60
  241.7 12.3 %reduce-scatter.2.cloned.1.call-done = bf16[352,256]{1,0:T(8,128)(2,1)} async-done(((bf16[352,1024]{1,0:T(8,128)(2,1)}), bf16[352,256]{1,0:T(8,128)(2,1)}) %reduce-scatter.2.cloned.1.call-update) | async-done | bytes 180240 | tf_op jit(solution)/shard_map/reduce_scatter | solution.py:166
  (102 shorter events, 9.9 us)
Async XLA Ops:
  7.2 63.2 %copy-start = (bf16[352,1024]{1,0:T(8,128)(2,1)S(1)}, bf16[352,1024]{1,0:T(8,128)(2,1)}, u32[]{:S(2)}) copy-start(bf16[352,1024]{1,0:T(8,128)(2,1)} %param.10) | copy-start | bytes 2162692
  7.2 34.6 %copy-start.12 = (bf16[1024,256]{1,0:T(8,128)(2,1)S(1)}, bf16[1024,256]{1,0:T(8,128)(2,1)}, u32[]{:S(2)}) copy-start(bf16[1024,256]{1,0:T(8,128)(2,1)} %param.12) | copy-start | bytes 1572868
  7.2 74.5 %all-gather.2.cloned.1.call-start = ((), (), s32[]{:S(2)}) async-start(), calls=%async_computation.1 | async-start | bytes 2621440 | tf_op jit(solution)/shard_map/all_gather | solution.py:85
  7.9 246.1 %reduce-scatter.2.cloned.1.call-start = ((), (), s32[]{:S(2)}) async-start(), calls=%async_computation.2 | async-start | bytes 901120 | tf_op jit(solution)/shard_map/reduce_scatter | solution.py:166
  8.0 19.7 %collective-permute-start.2 = (bf16[1024,256]{1,0:T(8,128)(2,1)}, bf16[1024,256]{1,0:T(8,128)(2,1)S(1)}, u32[]{:S(2)}, u32[]{:S(2)}) collective-permute-start(bf16[1024,256]{1,0:T(8,128)(2,1)} %param.12), channel_id=1, source_target_pairs={{0,1},{1,2},{2,3},{3,0},{4,5},{5,6},{6,7},{7,4},{8,9},{9,10},{10,1... | collective-permute-start | bytes 1572872 | tf_op jit(solution)/shard_map/ppermute | solution.py:18
  11.1 48.6 %collective-permute-start.3 = (bf16[1024,256]{1,0:T(8,128)(2,1)}, bf16[1024,256]{1,0:T(8,128)(2,1)S(1)}, u32[]{:S(2)}, u32[]{:S(2)}) collective-permute-start(bf16[1024,256]{1,0:T(8,128)(2,1)} %param.12), channel_id=1, source_target_pairs={{0,3},{1,0},{2,1},{3,2},{4,7},{5,4},{6,5},{7,6},{8,11},{9,8},{10,9... | collective-permute-start | bytes 1572872 | tf_op jit(solution)/shard_map/ppermute | solution.py:23
  27.7 42.6 %collective-permute-start.4 = (bf16[1024,256]{1,0:T(8,128)(2,1)S(1)}, bf16[1024,256]{1,0:T(8,128)(2,1)S(1)}, u32[]{:S(2)}, u32[]{:S(2)}) collective-permute-start(bf16[1024,256]{1,0:T(8,128)(2,1)S(1)} %collective-permute-done.2), channel_id=1, source_target_pairs={{0,1},{1,2},{2,3},{3,0},{4,5},{5,6},{6,7},{7,4},{8,9},{9,10},{10,1... | collective-permute-start | bytes 1572872 | tf_op jit(solution)/shard_map/ppermute | solution.py:18
  70.4 1.3 copy-start.5
  71.7 1.1 copy-start.3
  72.8 8.9 %copy-start.13 = (bf16[352,1024]{1,0:T(8,128)(2,1)S(1)}, bf16[352,1024]{1,0:T(8,128)(2,1)}, u32[]{:S(2)}) copy-start(bf16[352,1024]{1,0:T(8,128)(2,1)} %param.9) | copy-start | bytes 2162692
  73.0 0.9 copy-start.9
  84.3 1.1 copy-start.1
  84.5 1.2 copy-start.10
  85.7 14.1 %collective-permute-start = (bf16[352,1024]{1,0:T(8,128)(2,1)S(1)}, bf16[352,1024]{1,0:T(8,128)(2,1)S(1)}, u32[]{:S(2)}, u32[]{:S(2)}) collective-permute-start(bf16[352,1024]{1,0:T(8,128)(2,1)S(1)} %copy.19), channel_id=1, source_target_pairs={{0,4},{4,8},{8,12},{12,16},{16,20},{20,24},{24,28},{28,0},{1,5},{5... | collective-permute-start | bytes 2162696 | tf_op jit(solution)/shard_map/while/body/eval_jaxpr/ppermute | solution.py:33
  86.7 18.4 %collective-permute-start.1 = (bf16[352,1024]{1,0:T(8,128)(2,1)}, bf16[352,1024]{1,0:T(8,128)(2,1)S(1)}, u32[]{:S(2)}, u32[]{:S(2)}) collective-permute-start(bf16[352,1024]{1,0:T(8,128)(2,1)} %copy.20), channel_id=1, source_target_pairs={{0,4},{4,8},{8,12},{12,16},{16,20},{20,24},{24,28},{28,0},{1,5},{5... | collective-permute-start | bytes 2162696 | tf_op jit(solution)/shard_map/while/body/eval_jaxpr/ppermute | solution.py:33
  105.2 14.1 %collective-permute-start = (bf16[352,1024]{1,0:T(8,128)(2,1)S(1)}, bf16[352,1024]{1,0:T(8,128)(2,1)S(1)}, u32[]{:S(2)}, u32[]{:S(2)}) collective-permute-start(bf16[352,1024]{1,0:T(8,128)(2,1)S(1)} %copy.19), channel_id=1, source_target_pairs={{0,4},{4,8},{8,12},{12,16},{16,20},{20,24},{24,28},{28,0},{1,5},{5... | collective-permute-start | bytes 2162696 | tf_op jit(solution)/shard_map/while/body/eval_jaxpr/ppermute | solution.py:33
  106.1 18.4 %collective-permute-start.1 = (bf16[352,1024]{1,0:T(8,128)(2,1)}, bf16[352,1024]{1,0:T(8,128)(2,1)S(1)}, u32[]{:S(2)}, u32[]{:S(2)}) collective-permute-start(bf16[352,1024]{1,0:T(8,128)(2,1)} %copy.20), channel_id=1, source_target_pairs={{0,4},{4,8},{8,12},{12,16},{16,20},{20,24},{24,28},{28,0},{1,5},{5... | collective-permute-start | bytes 2162696 | tf_op jit(solution)/shard_map/while/body/eval_jaxpr/ppermute | solution.py:33
  124.6 13.4 %collective-permute-start = (bf16[352,1024]{1,0:T(8,128)(2,1)S(1)}, bf16[352,1024]{1,0:T(8,128)(2,1)S(1)}, u32[]{:S(2)}, u32[]{:S(2)}) collective-permute-start(bf16[352,1024]{1,0:T(8,128)(2,1)S(1)} %copy.19), channel_id=1, source_target_pairs={{0,4},{4,8},{8,12},{12,16},{16,20},{20,24},{24,28},{28,0},{1,5},{5... | collective-permute-start | bytes 2162696 | tf_op jit(solution)/shard_map/while/body/eval_jaxpr/ppermute | solution.py:33
  125.5 18.4 %collective-permute-start.1 = (bf16[352,1024]{1,0:T(8,128)(2,1)}, bf16[352,1024]{1,0:T(8,128)(2,1)S(1)}, u32[]{:S(2)}, u32[]{:S(2)}) collective-permute-start(bf16[352,1024]{1,0:T(8,128)(2,1)} %copy.20), channel_id=1, source_target_pairs={{0,4},{4,8},{8,12},{12,16},{16,20},{20,24},{24,28},{28,0},{1,5},{5... | collective-permute-start | bytes 2162696 | tf_op jit(solution)/shard_map/while/body/eval_jaxpr/ppermute | solution.py:33
  144.0 13.4 %collective-permute-start = (bf16[352,1024]{1,0:T(8,128)(2,1)S(1)}, bf16[352,1024]{1,0:T(8,128)(2,1)S(1)}, u32[]{:S(2)}, u32[]{:S(2)}) collective-permute-start(bf16[352,1024]{1,0:T(8,128)(2,1)S(1)} %copy.19), channel_id=1, source_target_pairs={{0,4},{4,8},{8,12},{12,16},{16,20},{20,24},{24,28},{28,0},{1,5},{5... | collective-permute-start | bytes 2162696 | tf_op jit(solution)/shard_map/while/body/eval_jaxpr/ppermute | solution.py:33
  145.0 18.4 %collective-permute-start.1 = (bf16[352,1024]{1,0:T(8,128)(2,1)}, bf16[352,1024]{1,0:T(8,128)(2,1)S(1)}, u32[]{:S(2)}, u32[]{:S(2)}) collective-permute-start(bf16[352,1024]{1,0:T(8,128)(2,1)} %copy.20), channel_id=1, source_target_pairs={{0,4},{4,8},{8,12},{12,16},{16,20},{20,24},{24,28},{28,0},{1,5},{5... | collective-permute-start | bytes 2162696 | tf_op jit(solution)/shard_map/while/body/eval_jaxpr/ppermute | solution.py:33
  163.5 13.4 %collective-permute-start = (bf16[352,1024]{1,0:T(8,128)(2,1)S(1)}, bf16[352,1024]{1,0:T(8,128)(2,1)S(1)}, u32[]{:S(2)}, u32[]{:S(2)}) collective-permute-start(bf16[352,1024]{1,0:T(8,128)(2,1)S(1)} %copy.19), channel_id=1, source_target_pairs={{0,4},{4,8},{8,12},{12,16},{16,20},{20,24},{24,28},{28,0},{1,5},{5... | collective-permute-start | bytes 2162696 | tf_op jit(solution)/shard_map/while/body/eval_jaxpr/ppermute | solution.py:33
  164.4 18.4 %collective-permute-start.1 = (bf16[352,1024]{1,0:T(8,128)(2,1)}, bf16[352,1024]{1,0:T(8,128)(2,1)S(1)}, u32[]{:S(2)}, u32[]{:S(2)}) collective-permute-start(bf16[352,1024]{1,0:T(8,128)(2,1)} %copy.20), channel_id=1, source_target_pairs={{0,4},{4,8},{8,12},{12,16},{16,20},{20,24},{24,28},{28,0},{1,5},{5... | collective-permute-start | bytes 2162696 | tf_op jit(solution)/shard_map/while/body/eval_jaxpr/ppermute | solution.py:33
  182.9 13.4 %collective-permute-start = (bf16[352,1024]{1,0:T(8,128)(2,1)S(1)}, bf16[352,1024]{1,0:T(8,128)(2,1)S(1)}, u32[]{:S(2)}, u32[]{:S(2)}) collective-permute-start(bf16[352,1024]{1,0:T(8,128)(2,1)S(1)} %copy.19), channel_id=1, source_target_pairs={{0,4},{4,8},{8,12},{12,16},{16,20},{20,24},{24,28},{28,0},{1,5},{5... | collective-permute-start | bytes 2162696 | tf_op jit(solution)/shard_map/while/body/eval_jaxpr/ppermute | solution.py:33
  183.9 18.4 %collective-permute-start.1 = (bf16[352,1024]{1,0:T(8,128)(2,1)}, bf16[352,1024]{1,0:T(8,128)(2,1)S(1)}, u32[]{:S(2)}, u32[]{:S(2)}) collective-permute-start(bf16[352,1024]{1,0:T(8,128)(2,1)} %copy.20), channel_id=1, source_target_pairs={{0,4},{4,8},{8,12},{12,16},{16,20},{20,24},{24,28},{28,0},{1,5},{5... | collective-permute-start | bytes 2162696 | tf_op jit(solution)/shard_map/while/body/eval_jaxpr/ppermute | solution.py:33
  202.4 13.4 %collective-permute-start = (bf16[352,1024]{1,0:T(8,128)(2,1)S(1)}, bf16[352,1024]{1,0:T(8,128)(2,1)S(1)}, u32[]{:S(2)}, u32[]{:S(2)}) collective-permute-start(bf16[352,1024]{1,0:T(8,128)(2,1)S(1)} %copy.19), channel_id=1, source_target_pairs={{0,4},{4,8},{8,12},{12,16},{16,20},{20,24},{24,28},{28,0},{1,5},{5... | collective-permute-start | bytes 2162696 | tf_op jit(solution)/shard_map/while/body/eval_jaxpr/ppermute | solution.py:33
  203.3 18.4 %collective-permute-start.1 = (bf16[352,1024]{1,0:T(8,128)(2,1)}, bf16[352,1024]{1,0:T(8,128)(2,1)S(1)}, u32[]{:S(2)}, u32[]{:S(2)}) collective-permute-start(bf16[352,1024]{1,0:T(8,128)(2,1)} %copy.20), channel_id=1, source_target_pairs={{0,4},{4,8},{8,12},{12,16},{16,20},{20,24},{24,28},{28,0},{1,5},{5... | collective-permute-start | bytes 2162696 | tf_op jit(solution)/shard_map/while/body/eval_jaxpr/ppermute | solution.py:33
  226.3 2.5 copy-start.11
  228.8 1.4 copy-start.2
  228.8 1.8 copy-start.7
  230.6 1.9 copy-start.4
  236.3 2.1 copy-start.6
  236.3 2.5 copy-start.8
Sparse Core Ops, SparseCore 0:
  9.6 72.1 all-gather.1
  232.6 21.3 reduce-scatter.1
